TPU v7x, 128 devices: a whole 4x4x4 slice. The times are simulated.
128 devices in a mesh: guide: 2 (over core), tensor: 16 (over y, x), batch: 4 (over z).
Axes of the slice: x: 4, y: 4, z: 4, core: 2. Of those that a mesh axis runs over, the one named last changes fastest.
Arguments:
- stream: bfloat16 [2, 512, 2048], P('guide', ('batch', 'tensor')), may hold values from -6 to 6
- attn_gain: float32 [2048], replicated, may hold values from 0.25 to 1.75
- w_qkv: bfloat16 [2048, 3072], P(None, 'tensor'), may hold values from -0.125 to 0.125
- cache_keys: bfloat16 [2, 512, 1024, 512], P('guide', ('batch', 'tensor')), may hold values from -600 to 600
- cache_values: bfloat16 [2, 512, 1024, 512], P('guide', ('batch', 'tensor')), may hold values from -6 to 6
- cache_len: int32 [2, 512], P('guide', ('batch', 'tensor')), may hold values from 1 to 1024, as said below
- w_out: bfloat16 [2048, 2048], P('tensor'), may hold values from -0.125 to 0.125
- mlp_gain: float32 [2048], replicated, may hold values from 0.25 to 1.75
- w_gate: bfloat16 [2048, 8192], P(None, 'tensor'), may hold values from -0.125 to 0.125
- w_up: bfloat16 [2048, 8192], P(None, 'tensor'), may hold values from -0.125 to 0.125
- w_down: bfloat16 [8192, 2048], P('tensor'), may hold values from -0.0625 to 0.0625
- final_gain: float32 [2048], replicated, may hold values from 0.25 to 1.75
- lm_head: bfloat16 [65536, 2048], P(('guide', 'tensor')), may hold values from -128 to 128
- next_gain: float32 [2048], replicated, may hold values from 0.25 to 1.75
- w_next: bfloat16 [2048, 3072], P(None, 'tensor'), may hold values from -0.125 to 0.125
- tenant_counts: int32 [4], replicated, may hold values from 1 to 256, 512 in all
- guide_level: int32 [4], replicated, may hold values from 4 to 16
Outputs:
- logprobs: float32 [512, 65536], P('batch', ('guide', 'tensor'))
- layer_out: bfloat16 [2, 512, 2048], P('guide', ('batch', 'tensor'))
- next_qkv: bfloat16 [2, 512, 3072], P('guide', 'batch', 'tensor')
Inputs may be any that keep to these rules, and one draw needn't show every extreme that they name: `cache_len`: in each branch some request has 1024 cached tokens.
All inputs are finite; a program needn't handle non-finite values.
Results may differ from a plain program's by a relative error of at most 0.024.
Values may be sent and summed in bfloat16 or wider, within the bound.
A program may use at most 128 MiB of HBM per device.

v0:
```python
import math
import jax
import jax.numpy as jnp
from jax import lax
from jax.sharding import PartitionSpec as P

D = 2048
HEADS = 32
KV_HEADS = 8
HEAD_DIM = 64
TENANTS = 4
EPSILON = 1e-05
ROPE_BASE = 500000.0
MASKED = -1e30


def from_partner(block, axis, bit):
    count = lax.axis_size(axis)
    route = []
    for low in range(count):
        high = low | 1 << bit
        if high != low and high < count:
            route += [(low, high), (high, low)]
    return lax.ppermute(block, axis, route)


def rms_norm(values, gain):
    widened = values.astype(jnp.float32)
    factor = lax.rsqrt(jnp.mean(widened * widened, axis=-1, keepdims=True) + EPSILON)
    return (widened * factor * gain).astype(jnp.bfloat16)


def scaled_freq(head_size):
    half_dim = head_size // 2
    steps_up = jnp.arange(half_dim, dtype=jnp.float32)
    base_freq = jnp.exp(steps_up * (-2.0 * math.log(ROPE_BASE) / head_size))
    wavelen = 2.0 * math.pi / base_freq
    smooth = (8192.0 / wavelen - 1.0) / 3.0
    middle = (1.0 - smooth) * base_freq / 32.0 + smooth * base_freq
    return jnp.where(
        wavelen < 2048.0, base_freq, jnp.where(wavelen > 8192.0, base_freq / 32.0, middle)
    )


def rotate(values, position):
    half_dim = values.shape[-1] // 2
    freq = scaled_freq(values.shape[-1])
    angle = position * freq
    cosine = jnp.cos(angle)
    sine = jnp.sin(angle)
    first = values[..., :half_dim].astype(jnp.float32)
    second = values[..., half_dim:].astype(jnp.float32)
    joined = jnp.concatenate(
        [first * cosine - second * sine, second * cosine + first * sine], axis=-1
    )
    return joined.astype(jnp.bfloat16)


def swiglu(normed, w_gate, w_up):
    gate = jnp.dot(normed, w_gate, preferred_element_type=jnp.float32)
    upward = jnp.dot(normed, w_up, preferred_element_type=jnp.float32)
    return (jax.nn.silu(gate) * upward).astype(jnp.bfloat16)


def attend(request_side, keys, values, lengths):
    count = request_side.shape[0]
    kv_width = KV_HEADS * HEAD_DIM
    per_group = HEADS // KV_HEADS
    scale = HEAD_DIM ** (-0.5)
    slot_count = keys.shape[1]
    position = lengths.astype(jnp.float32)[:, None, None]
    queries = rotate(request_side[:, :D].reshape(count, HEADS, HEAD_DIM), position)
    queries = queries.reshape(count, KV_HEADS, per_group, HEAD_DIM)
    new_keys = rotate(
        request_side[:, D : D + kv_width].reshape(count, KV_HEADS, HEAD_DIM), position
    )
    new_values = request_side[:, D + kv_width :].reshape(count, KV_HEADS, HEAD_DIM)
    keys_split = keys.reshape(count, slot_count, KV_HEADS, HEAD_DIM)
    values_split = values.reshape(count, slot_count, KV_HEADS, HEAD_DIM)
    fresh = (
        jnp.einsum("rkgd,rkd->rkg", queries, new_keys, preferred_element_type=jnp.float32) * scale
    )
    slots = jnp.arange(slot_count, dtype=jnp.int32)
    live_mask = (slots[None, :] < lengths[:, None])[:, None, None, :]
    scores = (
        jnp.einsum("rkgd,rlkd->rkgl", queries, keys_split, preferred_element_type=jnp.float32)
        * scale
    )
    scores = jnp.where(live_mask, scores, MASKED)
    peak = jnp.maximum(jnp.max(scores, axis=-1), fresh)
    expd = jnp.where(live_mask, jnp.exp(scores - peak[..., None]), 0.0)
    total = jnp.sum(expd, axis=-1)
    weighted = jnp.einsum(
        "rkgl,rlkd->rkgd",
        expd.astype(jnp.bfloat16),
        values_split,
        preferred_element_type=jnp.float32,
    )
    fresh_exp = jnp.exp(fresh - peak)
    total = total + fresh_exp
    fresh_prob = fresh_exp.astype(jnp.bfloat16).astype(jnp.float32)
    weighted = weighted + fresh_prob[..., None] * new_values.astype(jnp.float32)[:, :, None, :]
    return (weighted / total[..., None]).reshape(count, D).astype(jnp.bfloat16)


def local(
    stream,
    attn_gain,
    w_qkv,
    cache_keys,
    cache_values,
    cache_len,
    w_out,
    mlp_gain,
    w_gate,
    w_up,
    w_down,
    final_gain,
    lm_head,
    next_gain,
    w_next,
    tenant_counts,
    guide_level,
):
    own_rows = stream[0]
    projected = jnp.dot(
        lax.all_gather(rms_norm(own_rows, attn_gain), "tensor", axis=0, tiled=True),
        w_qkv,
        preferred_element_type=jnp.float32,
    ).astype(jnp.bfloat16)
    request_side = lax.all_to_all(projected, "tensor", split_axis=0, concat_axis=1, tiled=True)
    mixed = attend(request_side, cache_keys[0], cache_values[0], cache_len[0])
    head_side = lax.all_to_all(mixed, "tensor", split_axis=1, concat_axis=0, tiled=True)
    selected = head_side
    attn_share = lax.psum_scatter(
        jnp.dot(selected, w_out, preferred_element_type=jnp.float32).astype(jnp.bfloat16),
        "tensor",
        scatter_dimension=0,
        tiled=True,
    ).astype(jnp.float32)
    after_attn = (own_rows.astype(jnp.float32) + attn_share).astype(jnp.bfloat16)
    hidden = swiglu(
        lax.all_gather(rms_norm(after_attn, mlp_gain), "tensor", axis=0, tiled=True), w_gate, w_up
    )
    selected = hidden
    mlp_share = lax.psum_scatter(
        jnp.dot(selected, w_down, preferred_element_type=jnp.float32).astype(jnp.bfloat16),
        "tensor",
        scatter_dimension=0,
        tiled=True,
    ).astype(jnp.float32)
    layer_rows = (after_attn.astype(jnp.float32) + mlp_share).astype(jnp.bfloat16)
    all_out = lax.all_gather(layer_rows, "tensor", axis=0, tiled=True)
    next_rows = jnp.dot(
        rms_norm(all_out, next_gain), w_next, preferred_element_type=jnp.float32
    ).astype(jnp.bfloat16)
    final = rms_norm(all_out, final_gain)
    partner = from_partner(final, "guide", 0)
    is_cond = lax.axis_index("guide") == 0
    cond_rows = jnp.where(is_cond, final, partner)
    uncond_rows = jnp.where(is_cond, partner, final)
    batch_rows = final.shape[0]
    logits = lax.dot_general(
        jnp.concatenate([cond_rows, uncond_rows], axis=0),
        lm_head,
        (((1,), (1,)), ((), ())),
        preferred_element_type=jnp.float32,
    )
    cond_logits = logits[:batch_rows]
    uncond_logits = logits[batch_rows:]
    bounds = jnp.cumsum(tenant_counts)[:-1]
    request_ids = lax.axis_index("batch") * batch_rows + jnp.arange(batch_rows, dtype=jnp.int32)
    tenant = jnp.sum((request_ids[:, None] >= bounds[None, :]).astype(jnp.int32), axis=1)
    chosen = (tenant[:, None] == jnp.arange(TENANTS, dtype=jnp.int32)[None, :]).astype(jnp.float32)
    weight = jnp.sum(chosen * guide_level.astype(jnp.float32)[None, :], axis=1) * 0.25
    guided = uncond_logits + weight[:, None] * (cond_logits - uncond_logits)
    peak = lax.pmax(jnp.max(guided, axis=1), ("guide", "tensor"))
    mass = lax.psum(jnp.sum(jnp.exp(guided - peak[:, None]), axis=1), ("guide", "tensor"))
    logprobs = guided - peak[:, None] - jnp.log(mass)[:, None]
    return (logprobs, layer_rows[None], next_rows[None])


def solution(mesh):
    in_specs = (
        P("guide", ("batch", "tensor"), None),
        P(),
        P(None, "tensor"),
        P("guide", ("batch", "tensor"), None, None),
        P("guide", ("batch", "tensor"), None, None),
        P("guide", ("batch", "tensor")),
        P("tensor", None),
        P(),
        P(None, "tensor"),
        P(None, "tensor"),
        P("tensor", None),
        P(),
        P(("guide", "tensor"), None),
        P(),
        P(None, "tensor"),
        P(),
        P(),
    )
    out_specs = (
        P("batch", ("guide", "tensor")),
        P("guide", ("batch", "tensor"), None),
        P("guide", "batch", "tensor"),
    )
    return jax.shard_map(local, mesh=mesh, in_specs=in_specs, out_specs=out_specs, check_vma=False)
```

profile of v0, /device:TPU:1, one launch (start us, length us, event | category | flops | bytes accessed | tf_op | source)
XLA Modules:
  0.0 462.2 jit_solution(6862168536438569131)
XLA Ops:
  7.2 1.0 fusion.39
  8.2 0.8 fusion.41
  9.1 20.0 %all_gather.9 = bf16[128,2048]{1,0:T(8,128)(2,1)S(1)} all-gather(bf16[8,2048]{1,0:T(8,128)(2,1)S(1)} %fusion.41), channel_id=1, replica_groups=mesh['guide'=2,'tensor'=16,'batch'=4] {'tensor'}, dimensions={0}, use_global_device_ids=true | all-gather | bytes 557056 | tf_op jit(solution)/shard_map/all_gather | solution.py:127
  29.0 1.5 convolution_convert_fusion.3
  30.5 0.7 copy.32
  31.3 4.7 %all-to-all-start = ((bf16[16,8,192]{2,1,0:T(8,128)(2,1)}), bf16[16,8,192]{2,1,0:T(8,128)(2,1)S(1)}, u32[]{:S(2)}, u32[]{:S(2)}) async-start(bf16[16,8,192]{2,1,0:T(8,128)(2,1)} %bitcast.3), calls=%async_computation | async-start | bytes 131072 | tf_op jit(solution)/shard_map/all_to_all | solution.py:131
  36.1 0.1 multiply_cosine_fusion
  36.2 0.1 iota_compare_fusion
  36.3 11.4 %copy.34 = bf16[1,8,1024,512]{2,3,1,0:T(8,128)(2,1)} copy(bf16[1,8,1024,512]{3,2,1,0:T(8,128)(2,1)} %param.20) | data formatting | bytes 16777216 | tf_op args[3]
  47.7 11.5 %copy.35 = bf16[1,8,1024,512]{2,3,1,0:T(8,128)(2,1)} copy(bf16[1,8,1024,512]{3,2,1,0:T(8,128)(2,1)} %param.21) | data formatting | bytes 16777216 | tf_op args[4]
  59.2 0.1 all_to_all.29
  59.3 0.1 reshape.189
  59.4 0.1 reshape.188
  59.5 0.1 fusion.44
  59.6 0.1 fusion.31
  59.7 0.1 maximum_bitcast_fusion
  59.8 0.3 fusion.48
  60.1 4.8 %fusion.57 = (f32[8,8,4]{2,1,0:T(8,128)S(1)}, f32[8,8,4,1024]{3,2,1,0:T(4,128)S(1)}) fusion(bf16[8,1024,8,64]{1,3,2,0:T(8,128)(2,1)} %bitcast.42, bf16[8,8,4,32]{3,2,1,0:T(4,128)(2,1)S(1)} %bitcast.47, bf16[8,8,4,32]{3,2,1,0:T(4,128)(2,1)S(1)} %bitcast.45, pred[8,1024]{1,0:T(8,128)(4,1)S(1)} %iota_compare_fusion), kind=kOutput, calls=%fused_computation.103 | convolution fusion | flops 34406144 | bytes 9479168 | tf_op jit(solution)/shard_map/rkgd,rlkd->rkgl/dot_general | solution.py:86
  64.8 0.6 fusion.16
  65.5 0.1 reshape.192
  65.6 5.8 %fusion.5 = bf16[8,8,4,64]{3,2,1,0:T(4,128)(2,1)S(1)} fusion(bf16[8,1024,8,64]{1,3,2,0:T(8,128)(2,1)} %bitcast.43, f32[8,8,4,1024]{3,2,1,0:T(4,128)S(1)} %get-tuple-element.20, f32[8,8,4]{2,1,0:T(8,128)S(1)} %multiply_maximum_fusion, pred[8,1024]{1,0:T(8,128)(4,1)S(1)} %iota_compare_fusion, f32[8,8,4]{2,1,0:T(8,128)S(1)} %get-tuple-element.12, ...), kind=kOutput, calls=%fused_computation.12 | convolution fusion | flops 34406400 | bytes 9497600 | tf_op jit(solution)/shard_map/rkgl,rlkd->rkgd/dot_general | solution.py:93
  71.3 0.1 convert_element_type.124
  71.5 12.9 %all_to_all.35 = bf16[8,16,128]{2,0,1:T(8,128)(2,1)S(1)} all-to-all(bf16[8,16,128]{2,0,1:T(8,128)(2,1)S(1)} %copy.36), channel_id=1, replica_groups=mesh['guide'=2,'tensor'=16,'batch'=4] {'tensor'}, dimensions={1} | all-to-all | bytes 65536 | tf_op jit(solution)/shard_map/all_to_all | solution.py:133
  84.4 2.1 convolution_convert_fusion.1
  86.6 0.6 dynamic-slice
  87.8 88.3 %all-reduce.5.cloned.1.call-done = bf16[128,2048]{1,0:T(8,128)(2,1)} async-done(((bf16[128,2048]{1,0:T(8,128)(2,1)}), bf16[128,2048]{1,0:T(8,128)(2,1)}) %all-reduce.5.cloned.1.call-update) | async-done | bytes 524304
  176.1 0.9 fusion.35
  177.0 0.1 fusion.37
  177.1 17.4 %all_gather.10 = bf16[128,2048]{1,0:T(8,128)(2,1)S(1)} all-gather(bf16[8,2048]{1,0:T(8,128)(2,1)S(1)} %fusion.37), channel_id=1, replica_groups=mesh['guide'=2,'tensor'=16,'batch'=4] {'tensor'}, dimensions={0}, use_global_device_ids=true | all-gather | bytes 557056 | tf_op jit(solution)/shard_map/all_gather | solution.py:143
  194.5 2.0 fusion.58
  196.6 3.2 convolution_convert_fusion
  199.9 0.2 reduce-window.4
  200.1 0.1 convert_reduce_fusion
  200.2 89.2 %all-reduce.7.cloned.1.call-done = bf16[128,2048]{1,0:T(8,128)(2,1)} async-done(((bf16[128,2048]{1,0:T(8,128)(2,1)}), bf16[128,2048]{1,0:T(8,128)(2,1)}) %all-reduce.7.cloned.1.call-update) | async-done | bytes 524304
  289.3 0.8 fusion.38
  290.1 17.4 %all_gather.11 = bf16[128,2048]{1,0:T(8,128)(2,1)S(1)} all-gather(bf16[8,2048]{1,0:T(8,128)(2,1)S(1)} %fusion.38), channel_id=1, replica_groups=mesh['guide'=2,'tensor'=16,'batch'=4] {'tensor'}, dimensions={0}, use_global_device_ids=true | all-gather | bytes 557056 | tf_op jit(solution)/shard_map/all_gather | solution.py:153
  307.5 0.2 fusion.9
  307.7 0.2 fusion.7
  307.9 8.1 %collective-permute-start = (bf16[128,2048]{1,0:T(8,128)(2,1)S(1)}, bf16[128,2048]{1,0:T(8,128)(2,1)}, u32[]{:S(2)}, u32[]{:S(2)}) collective-permute-start(bf16[128,2048]{1,0:T(8,128)(2,1)S(1)} %fusion.7), channel_id=1, source_target_pairs={{0,64},{64,0},{1,65},{65,1},{2,66},{66,2},{3,67},{67,3},{4,68},{68... | collective-permute-start | bytes 1572872 | tf_op jit(solution)/shard_map/ppermute | solution.py:24
  316.1 0.1 select_reduce_fusion
  316.1 2.2 fusion.6
  318.4 1.4 broadcast_select_fusion.1
  319.8 5.7 %fusion.12 = f32[256,2048]{1,0:T(8,128)S(1)} fusion(bf16[2048,2048]{1,0:T(8,128)(2,1)} %param.29, bf16[128,2048]{1,0:T(8,128)(2,1)S(1)} %get-tuple-element.8, bf16[128,2048]{1,0:T(8,128)(2,1)S(1)} %get-tuple-element.7), kind=kOutput, calls=%fused_computation.22 | convolution fusion | flops 2149580800 | bytes 11534336 | tf_op jit(solution)/shard_map/dot_general | solution.py:163
  325.5 0.4 fusion.54
  326.0 65.0 %pmax.7 = f32[128]{0:T(128)S(1)} all-reduce(f32[128]{0:T(128)S(1)} %get-tuple-element.3), channel_id=1, replica_groups=mesh['guide'=2,'tensor'=16,'batch'=4] {'guide','tensor'}, use_global_device_ids=true, to_apply=%region_11.12 | all-reduce | flops 128 | bytes 1024 | tf_op jit(solution)/shard_map/pmax | solution.py:177
  391.0 0.3 exponential_reduce_fusion
  391.3 62.9 %psum.7 = f32[128]{0:T(128)S(1)} all-reduce(f32[128]{0:T(128)S(1)} %exponential_reduce_fusion), channel_id=1, replica_groups=mesh['guide'=2,'tensor'=16,'batch'=4] {'guide','tensor'}, use_global_device_ids=true, to_apply=%region_13.14 | all-reduce | flops 128 | bytes 1024 | tf_op jit(solution)/shard_map/psum | solution.py:178
  454.2 1.1 subtract_subtract_fusion
  (42 shorter events, 0.3 us)
Async XLA Ops:
  7.2 189.4 %copy-start = (bf16[512,2048]{1,0:T(8,128)(2,1)S(1)}, bf16[512,2048]{1,0:T(8,128)(2,1)}, u32[]{:S(2)}) copy-start(bf16[512,2048]{1,0:T(8,128)(2,1)} %param.27) | copy-start | bytes 6291460
  7.2 28.9 %copy-start.5 = (s32[1,8]{1,0:T(1,128)S(1)}, s32[1,8]{1,0:T(1,128)}, u32[]{:S(2)}) copy-start(s32[1,8]{1,0:T(1,128)} %param.22) | copy-start | bytes 100
  31.3 27.9 %all-to-all-start = ((bf16[16,8,192]{2,1,0:T(8,128)(2,1)}), bf16[16,8,192]{2,1,0:T(8,128)(2,1)S(1)}, u32[]{:S(2)}, u32[]{:S(2)}) async-start(bf16[16,8,192]{2,1,0:T(8,128)(2,1)} %bitcast.3), calls=%async_computation | async-start | bytes 131072 | tf_op jit(solution)/shard_map/all_to_all | solution.py:131
  36.0 140.2 %all-reduce.5.cloned.1.call-start = ((), (), s32[]{:S(2)}) async-start(), calls=%async_computation.2 | async-start | bytes 1048576
  65.5 21.1 %copy-start.9 = (u32[128]{0:T(128)S(1)}, u32[128]{0:T(128)}, u32[]{:S(2)}) copy-start(u32[128]{0:T(128)} %constant.67) | copy-start | bytes 1540
  65.5 110.6 %copy-start.1 = (bf16[1,8,2048]{2,1,0:T(8,128)(2,1)S(1)}, bf16[1,8,2048]{2,1,0:T(8,128)(2,1)}, u32[]{:S(2)}) copy-start(bf16[1,8,2048]{2,1,0:T(8,128)(2,1)} %param.17) | copy-start | bytes 98308
  65.6 111.5 %copy-start.4 = (f32[2048]{0:T(1024)S(1)}, f32[2048]{0:T(1024)}, u32[]{:S(2)}) copy-start(f32[2048]{0:T(1024)} %param.24) | copy-start | bytes 24580
  86.5 202.8 %all-reduce.7.cloned.1.call-start = ((), (), s32[]{:S(2)}) async-start(), calls=%async_computation.3 | async-start | bytes 1048576
  196.6 3.3 copy-start.7
  196.6 111.1 %copy-start.3 = (f32[2048]{0:T(1024)S(1)}, f32[2048]{0:T(1024)}, u32[]{:S(2)}) copy-start(f32[2048]{0:T(1024)} %param.28) | copy-start | bytes 24580
  199.8 116.2 %copy-start.8 = (s32[4]{0:T(128)S(1)}, s32[4]{0:T(128)}, u32[]{:S(2)}) copy-start(s32[4]{0:T(128)} %param.33) | copy-start | bytes 52
  199.8 116.3 %copy-start.6 = (f32[2048]{0:T(1024)S(1)}, f32[2048]{0:T(1024)}, u32[]{:S(2)}) copy-start(f32[2048]{0:T(1024)} %param.30) | copy-start | bytes 24580
  290.1 29.7 %copy-start.2 = (bf16[8,2048]{1,0:T(8,128)(2,1)}, bf16[8,2048]{1,0:T(8,128)(2,1)S(1)}, u32[]{:S(2)}) copy-start(bf16[8,2048]{1,0:T(8,128)(2,1)S(1)} %fusion.38) | copy-start | bytes 98308
  307.9 10.4 %collective-permute-start = (bf16[128,2048]{1,0:T(8,128)(2,1)S(1)}, bf16[128,2048]{1,0:T(8,128)(2,1)}, u32[]{:S(2)}, u32[]{:S(2)}) collective-permute-start(bf16[128,2048]{1,0:T(8,128)(2,1)S(1)} %fusion.7), channel_id=1, source_target_pairs={{0,64},{64,0},{1,65},{65,1},{2,66},{66,2},{3,67},{67,3},{4,68},{68... | collective-permute-start | bytes 1572872 | tf_op jit(solution)/shard_map/ppermute | solution.py:24
Sparse Core Ops, SparseCore 0:
  86.7 89.4 all-reduce.4
  200.0 89.2 all-reduce.6
where the time goes:
time: 464 us; the launch traced here: 462 us
  blocking collectives  196 us (42%)
  waiting for transfers between devices  178 us (38%)
  matrix products  27.7 us (6%)
  local copies, waits for them, and re-layouts  24.8 us (5%)
  between operations  14.9 us (3%)
  starting transfers between devices  12.9 us (3%)
  other arithmetic  8.77 us (2%)
    unnamed x4, waiting for transfers between devices  177 us
    pmax x1, blocking collectives, local(): peak = lax.pmax(jnp.max(guided, axis=1), ('guide', 'tensor'))  65 us
    psum x1, blocking collectives, local(): lax.psum(jnp.sum(jnp.exp(guided - peak[:, None]), axis=1), ('guide', 'ten...  62.9 us
    unnamed x23, local copies, waits for them, and re-layouts  23.5 us
    all_gather x1, blocking collectives, local(): lax.all_gather(rms_norm(own_rows, attn_gain), 'tensor', axis=0, tiled=True)  20 us
    all_gather x1, blocking collectives, local(): all_out = lax.all_gather(layer_rows, 'tensor', axis=0, tiled=True)  17.4 us
    all_gather x1, blocking collectives, local(): lax.all_gather(rms_norm(after_attn, mlp_gain), 'tensor', axis=0, tiled=True)  17.4 us
    all_to_all x1, blocking collectives, local(): lax.all_to_all(mixed, 'tensor', split_axis=1, concat_axis=0, tiled=True)  12.9 us
  transfers between devices with their start and end apart: 4, of which 2 were waited for; matrix products, arithmetic and copies ran while one was open for 6% of the time, Pallas kernels for 0%

commit v1 on v0

--- a/solution.py
+++ b/solution.py
@@ -175,7 +175,7 @@
     weight = jnp.sum(chosen * guide_level.astype(jnp.float32)[None, :], axis=1) * 0.25
     guided = uncond_logits + weight[:, None] * (cond_logits - uncond_logits)
     peak = lax.pmax(jnp.max(guided, axis=1), ("guide", "tensor"))
-    mass = lax.psum(jnp.sum(jnp.exp(guided - peak[:, None]), axis=1), ("guide", "tensor"))
+    mass = lax.psum(lax.psum(jnp.sum(jnp.exp(guided - peak[:, None]), axis=1), "tensor"), "guide")
     logprobs = guided - peak[:, None] - jnp.log(mass)[:, None]
     return (logprobs, layer_rows[None], next_rows[None])
 

time: 464 us -> 439 us (0.946)
  blocking collectives: 196 us -> 171 us
    psum x1 -> x2, blocking collectives: 62.9 us -> 38.2 us  [the longest x1 28.6 us: local(): lax.psum(jnp.sum(jnp.exp(guided - peak[:, None]), axis=1), 'tensor')]
where the time goes in v1:
time: 439 us; the launch traced here: 437 us
  waiting for transfers between devices  178 us (41%)
  blocking collectives  171 us (39%)
  matrix products  27.7 us (6%)
  local copies, waits for them, and re-layouts  24.8 us (6%)
  between operations  14.9 us (3%)
  starting transfers between devices  12.9 us (3%)
  other arithmetic  8.77 us (2%)
    unnamed x4, waiting for transfers between devices  177 us
    pmax x1, blocking collectives, local(): peak = lax.pmax(jnp.max(guided, axis=1), ('guide', 'tensor'))  65 us
    psum x1, blocking collectives, local(): lax.psum(jnp.sum(jnp.exp(guided - peak[:, None]), axis=1), 'tensor')  28.6 us
    unnamed x23, local copies, waits for them, and re-layouts  23.5 us
    all_gather x1, blocking collectives, local(): lax.all_gather(rms_norm(own_rows, attn_gain), 'tensor', axis=0, tiled=True)  20 us
    all_gather x1, blocking collectives, local(): all_out = lax.all_gather(layer_rows, 'tensor', axis=0, tiled=True)  17.4 us
    all_gather x1, blocking collectives, local(): lax.all_gather(rms_norm(after_attn, mlp_gain), 'tensor', axis=0, tiled=True)  17.4 us
    all_to_all x1, blocking collectives, local(): lax.all_to_all(mixed, 'tensor', split_axis=1, concat_axis=0, tiled=True)  12.9 us
  transfers between devices with their start and end apart: 4, of which 2 were waited for; matrix products, arithmetic and copies ran while one was open for 6% of the time, Pallas kernels for 0%

profile of v1, /device:TPU:1, one launch (start us, length us, event | category | flops | bytes accessed | tf_op | source)
XLA Modules:
  0.0 437.5 jit_solution(3058570671412432433)
XLA Ops:
  7.2 1.0 fusion.39
  8.2 0.8 fusion.41
  9.1 20.0 %all_gather.9 = bf16[128,2048]{1,0:T(8,128)(2,1)S(1)} all-gather(bf16[8,2048]{1,0:T(8,128)(2,1)S(1)} %fusion.41), channel_id=1, replica_groups=mesh['guide'=2,'tensor'=16,'batch'=4] {'tensor'}, dimensions={0}, use_global_device_ids=true | all-gather | bytes 557056 | tf_op jit(solution)/shard_map/all_gather | solution.py:127
  29.0 1.5 convolution_convert_fusion.3
  30.5 0.7 copy.32
  31.3 4.7 %all-to-all-start = ((bf16[16,8,192]{2,1,0:T(8,128)(2,1)}), bf16[16,8,192]{2,1,0:T(8,128)(2,1)S(1)}, u32[]{:S(2)}, u32[]{:S(2)}) async-start(bf16[16,8,192]{2,1,0:T(8,128)(2,1)} %bitcast.3), calls=%async_computation | async-start | bytes 131072 | tf_op jit(solution)/shard_map/all_to_all | solution.py:131
  36.1 0.1 multiply_cosine_fusion
  36.2 0.1 iota_compare_fusion
  36.3 11.4 %copy.34 = bf16[1,8,1024,512]{2,3,1,0:T(8,128)(2,1)} copy(bf16[1,8,1024,512]{3,2,1,0:T(8,128)(2,1)} %param.20) | data formatting | bytes 16777216 | tf_op args[3]
  47.7 11.5 %copy.35 = bf16[1,8,1024,512]{2,3,1,0:T(8,128)(2,1)} copy(bf16[1,8,1024,512]{3,2,1,0:T(8,128)(2,1)} %param.21) | data formatting | bytes 16777216 | tf_op args[4]
  59.2 0.1 all_to_all.29
  59.3 0.1 reshape.189
  59.4 0.1 reshape.188
  59.5 0.1 fusion.44
  59.6 0.1 fusion.31
  59.7 0.1 maximum_bitcast_fusion
  59.8 0.3 fusion.48
  60.1 4.8 %fusion.57 = (f32[8,8,4]{2,1,0:T(8,128)S(1)}, f32[8,8,4,1024]{3,2,1,0:T(4,128)S(1)}) fusion(bf16[8,1024,8,64]{1,3,2,0:T(8,128)(2,1)} %bitcast.42, bf16[8,8,4,32]{3,2,1,0:T(4,128)(2,1)S(1)} %bitcast.47, bf16[8,8,4,32]{3,2,1,0:T(4,128)(2,1)S(1)} %bitcast.45, pred[8,1024]{1,0:T(8,128)(4,1)S(1)} %iota_compare_fusion), kind=kOutput, calls=%fused_computation.103 | convolution fusion | flops 34406144 | bytes 9479168 | tf_op jit(solution)/shard_map/rkgd,rlkd->rkgl/dot_general | solution.py:86
  64.8 0.6 fusion.16
  65.6 5.8 %fusion.5 = bf16[8,8,4,64]{3,2,1,0:T(4,128)(2,1)S(1)} fusion(bf16[8,1024,8,64]{1,3,2,0:T(8,128)(2,1)} %bitcast.43, f32[8,8,4,1024]{3,2,1,0:T(4,128)S(1)} %get-tuple-element.20, f32[8,8,4]{2,1,0:T(8,128)S(1)} %multiply_maximum_fusion, pred[8,1024]{1,0:T(8,128)(4,1)S(1)} %iota_compare_fusion, f32[8,8,4]{2,1,0:T(8,128)S(1)} %get-tuple-element.12, ...), kind=kOutput, calls=%fused_computation.12 | convolution fusion | flops 34406400 | bytes 9497600 | tf_op jit(solution)/shard_map/rkgl,rlkd->rkgd/dot_general | solution.py:93
  71.3 0.1 convert_element_type.124
  71.5 12.9 %all_to_all.35 = bf16[8,16,128]{2,0,1:T(8,128)(2,1)S(1)} all-to-all(bf16[8,16,128]{2,0,1:T(8,128)(2,1)S(1)} %copy.36), channel_id=1, replica_groups=mesh['guide'=2,'tensor'=16,'batch'=4] {'tensor'}, dimensions={1} | all-to-all | bytes 65536 | tf_op jit(solution)/shard_map/all_to_all | solution.py:133
  84.4 2.1 convolution_convert_fusion.1
  86.6 0.6 dynamic-slice
  87.8 88.3 %all-reduce.5.cloned.1.call-done = bf16[128,2048]{1,0:T(8,128)(2,1)} async-done(((bf16[128,2048]{1,0:T(8,128)(2,1)}), bf16[128,2048]{1,0:T(8,128)(2,1)}) %all-reduce.5.cloned.1.call-update) | async-done | bytes 524304
  176.1 0.9 fusion.35
  177.0 0.1 fusion.37
  177.1 17.4 %all_gather.10 = bf16[128,2048]{1,0:T(8,128)(2,1)S(1)} all-gather(bf16[8,2048]{1,0:T(8,128)(2,1)S(1)} %fusion.37), channel_id=1, replica_groups=mesh['guide'=2,'tensor'=16,'batch'=4] {'tensor'}, dimensions={0}, use_global_device_ids=true | all-gather | bytes 557056 | tf_op jit(solution)/shard_map/all_gather | solution.py:143
  194.5 2.0 fusion.58
  196.6 3.2 convolution_convert_fusion
  199.9 0.2 reduce-window.4
  200.1 0.1 convert_reduce_fusion
  200.2 89.2 %all-reduce.7.cloned.1.call-done = bf16[128,2048]{1,0:T(8,128)(2,1)} async-done(((bf16[128,2048]{1,0:T(8,128)(2,1)}), bf16[128,2048]{1,0:T(8,128)(2,1)}) %all-reduce.7.cloned.1.call-update) | async-done | bytes 524304
  289.3 0.8 fusion.38
  290.1 17.4 %all_gather.11 = bf16[128,2048]{1,0:T(8,128)(2,1)S(1)} all-gather(bf16[8,2048]{1,0:T(8,128)(2,1)S(1)} %fusion.38), channel_id=1, replica_groups=mesh['guide'=2,'tensor'=16,'batch'=4] {'tensor'}, dimensions={0}, use_global_device_ids=true | all-gather | bytes 557056 | tf_op jit(solution)/shard_map/all_gather | solution.py:153
  307.5 0.2 fusion.9
  307.7 0.2 fusion.7
  307.9 8.1 %collective-permute-start = (bf16[128,2048]{1,0:T(8,128)(2,1)S(1)}, bf16[128,2048]{1,0:T(8,128)(2,1)}, u32[]{:S(2)}, u32[]{:S(2)}) collective-permute-start(bf16[128,2048]{1,0:T(8,128)(2,1)S(1)} %fusion.7), channel_id=1, source_target_pairs={{0,64},{64,0},{1,65},{65,1},{2,66},{66,2},{3,67},{67,3},{4,68},{68... | collective-permute-start | bytes 1572872 | tf_op jit(solution)/shard_map/ppermute | solution.py:24
  316.1 0.1 select_reduce_fusion
  316.1 2.2 fusion.6
  318.4 1.4 broadcast_select_fusion.1
  319.8 5.7 %fusion.12 = f32[256,2048]{1,0:T(8,128)S(1)} fusion(bf16[2048,2048]{1,0:T(8,128)(2,1)} %param.29, bf16[128,2048]{1,0:T(8,128)(2,1)S(1)} %get-tuple-element.8, bf16[128,2048]{1,0:T(8,128)(2,1)S(1)} %get-tuple-element.7), kind=kOutput, calls=%fused_computation.22 | convolution fusion | flops 2149580800 | bytes 11534336 | tf_op jit(solution)/shard_map/dot_general | solution.py:163
  325.5 0.4 fusion.54
  326.0 65.0 %pmax.7 = f32[128]{0:T(128)S(1)} all-reduce(f32[128]{0:T(128)S(1)} %get-tuple-element.3), channel_id=1, replica_groups=mesh['guide'=2,'tensor'=16,'batch'=4] {'guide','tensor'}, use_global_device_ids=true, to_apply=%region_11.12 | all-reduce | flops 128 | bytes 1024 | tf_op jit(solution)/shard_map/pmax | solution.py:177
  391.0 0.3 exponential_reduce_fusion
  391.3 28.6 %psum.14 = f32[128]{0:T(128)S(1)} all-reduce(f32[128]{0:T(128)S(1)} %exponential_reduce_fusion), channel_id=1, replica_groups=mesh['guide'=2,'tensor'=16,'batch'=4] {'tensor'}, use_global_device_ids=true, to_apply=%region_13.14 | all-reduce | flops 128 | bytes 1024 | tf_op jit(solution)/shard_map/psum | solution.py:178
  420.0 9.5 %psum.15 = f32[128]{0:T(128)S(1)} all-reduce(f32[128]{0:T(128)S(1)} %psum.14), channel_id=1, replica_groups=mesh['guide'=2,'tensor'=16,'batch'=4] {'guide'}, use_global_device_ids=true, to_apply=%region_14.15 | all-reduce | flops 128 | bytes 1024 | tf_op jit(solution)/shard_map/psum | solution.py:178
  429.5 1.1 subtract_subtract_fusion
  (43 shorter events, 0.4 us)
Async XLA Ops:
  7.2 189.4 %copy-start = (bf16[512,2048]{1,0:T(8,128)(2,1)S(1)}, bf16[512,2048]{1,0:T(8,128)(2,1)}, u32[]{:S(2)}) copy-start(bf16[512,2048]{1,0:T(8,128)(2,1)} %param.27) | copy-start | bytes 6291460
  7.2 28.9 %copy-start.5 = (s32[1,8]{1,0:T(1,128)S(1)}, s32[1,8]{1,0:T(1,128)}, u32[]{:S(2)}) copy-start(s32[1,8]{1,0:T(1,128)} %param.22) | copy-start | bytes 100
  31.3 27.9 %all-to-all-start = ((bf16[16,8,192]{2,1,0:T(8,128)(2,1)}), bf16[16,8,192]{2,1,0:T(8,128)(2,1)S(1)}, u32[]{:S(2)}, u32[]{:S(2)}) async-start(bf16[16,8,192]{2,1,0:T(8,128)(2,1)} %bitcast.3), calls=%async_computation | async-start | bytes 131072 | tf_op jit(solution)/shard_map/all_to_all | solution.py:131
  36.0 140.2 %all-reduce.5.cloned.1.call-start = ((), (), s32[]{:S(2)}) async-start(), calls=%async_computation.2 | async-start | bytes 1048576
  65.5 21.1 %copy-start.9 = (u32[128]{0:T(128)S(1)}, u32[128]{0:T(128)}, u32[]{:S(2)}) copy-start(u32[128]{0:T(128)} %constant.67) | copy-start | bytes 1540
  65.5 110.6 %copy-start.1 = (bf16[1,8,2048]{2,1,0:T(8,128)(2,1)S(1)}, bf16[1,8,2048]{2,1,0:T(8,128)(2,1)}, u32[]{:S(2)}) copy-start(bf16[1,8,2048]{2,1,0:T(8,128)(2,1)} %param.17) | copy-start | bytes 98308
  65.6 111.5 %copy-start.4 = (f32[2048]{0:T(1024)S(1)}, f32[2048]{0:T(1024)}, u32[]{:S(2)}) copy-start(f32[2048]{0:T(1024)} %param.24) | copy-start | bytes 24580
  86.5 202.8 %all-reduce.7.cloned.1.call-start = ((), (), s32[]{:S(2)}) async-start(), calls=%async_computation.3 | async-start | bytes 1048576
  196.6 3.3 copy-start.7
  196.6 111.1 %copy-start.3 = (f32[2048]{0:T(1024)S(1)}, f32[2048]{0:T(1024)}, u32[]{:S(2)}) copy-start(f32[2048]{0:T(1024)} %param.28) | copy-start | bytes 24580
  199.8 116.2 %copy-start.8 = (s32[4]{0:T(128)S(1)}, s32[4]{0:T(128)}, u32[]{:S(2)}) copy-start(s32[4]{0:T(128)} %param.33) | copy-start | bytes 52
  199.8 116.3 %copy-start.6 = (f32[2048]{0:T(1024)S(1)}, f32[2048]{0:T(1024)}, u32[]{:S(2)}) copy-start(f32[2048]{0:T(1024)} %param.30) | copy-start | bytes 24580
  290.1 29.7 %copy-start.2 = (bf16[8,2048]{1,0:T(8,128)(2,1)}, bf16[8,2048]{1,0:T(8,128)(2,1)S(1)}, u32[]{:S(2)}) copy-start(bf16[8,2048]{1,0:T(8,128)(2,1)S(1)} %fusion.38) | copy-start | bytes 98308
  307.9 10.4 %collective-permute-start = (bf16[128,2048]{1,0:T(8,128)(2,1)S(1)}, bf16[128,2048]{1,0:T(8,128)(2,1)}, u32[]{:S(2)}, u32[]{:S(2)}) collective-permute-start(bf16[128,2048]{1,0:T(8,128)(2,1)S(1)} %fusion.7), channel_id=1, source_target_pairs={{0,64},{64,0},{1,65},{65,1},{2,66},{66,2},{3,67},{67,3},{4,68},{68... | collective-permute-start | bytes 1572872 | tf_op jit(solution)/shard_map/ppermute | solution.py:24
Sparse Core Ops, SparseCore 0:
  86.7 89.4 all-reduce.4
  200.0 89.2 all-reduce.6
